TPU v7x, 32 devices: a whole 2x2x4 slice. The times are simulated.
32 devices in a mesh: bond: 8 (over z, x), sector: 4 (over y, core).
Axes of the slice: x: 2, y: 2, z: 4, core: 2. Of those that a mesh axis runs over, the one named last changes fastest.
Arguments:
- theta: bfloat16 [4, 768, 768], P('sector'), may hold values from -80 to 80
- sector_dims: int32 [4], P('sector'), may hold values from 1 to 768, 2304 in all
- right_dims: int32 [4], P('sector'), may hold values from 1 to 768, 2304 in all
- env_left: bfloat16 [16, 4, 768, 768], P('bond', 'sector'), may hold values from -0.21875 to 0.21875
- env_right: bfloat16 [16, 4, 768, 768], P('bond', 'sector'), may hold values from -0.21875 to 0.21875
- mpo_on: int32 [16], P('bond'), may hold values 0 or 1
- mpo_coef: float32 [16], P('bond'), may hold values from -3 to 3
- mix_index: int32 [16, 3], P('bond'), may hold values from 0 to 7
- weight_table: float32 [8], replicated, may hold values from -3 to 3
Outputs:
- matvec: bfloat16 [4, 768, 768], P('sector', 'bond')
- env_next: bfloat16 [16, 4, 768, 768], P('bond', 'sector')
All inputs are finite; a program needn't handle non-finite values. No bound on the sum of `sector_dims` or of `right_dims` or of `mpo_on` on one device may be relied on, other than what follows from the above.
Results may differ from a plain program's by a relative error of at most 0.008.
Values may be sent and summed in bfloat16 or wider, within the bound.
No kernel may reach another device: no remote copies, remote signals or barrier semaphores. Data moves between devices by JAX's collectives and lax.ppermute only.
A program may use at most 64 MiB of HBM per device.

v0:
```python
import math

import jax
import jax.numpy as jnp
from jax import lax
from jax.sharding import PartitionSpec as P


def padded(shard, sides, width):
    for axis, dim in sides:
        peers, length = (lax.axis_size(axis), shard.shape[dim])
        up = [(i, (i + 1) % peers) for i in range(peers - 1)]
        down = [(j, i) for i, j in up]
        last = lax.slice_in_dim(shard, length - width, length, axis=dim)
        first = lax.slice_in_dim(shard, 0, width, axis=dim)
        before = lax.ppermute(last, axis, up)
        after = lax.ppermute(first, axis, down)
        shard = jnp.concatenate([before, shard, after], axis=dim)
    return shard


def on_device(
    theta, sector_dims, right_dims, env_left, env_right, mpo_on, mpo_coef, mix_index, weight_table
):
    states = theta.shape[1]
    bond_local = env_left.shape[0]
    index = jnp.arange(states, dtype=jnp.int32)
    row_flag = index < sector_dims[0]
    col_flag = index < right_dims[0]
    row_live = row_flag.astype(jnp.float32)
    col_live = col_flag.astype(jnp.float32)
    live = jnp.where(row_flag[:, None] & col_flag[None, :], theta[0], jnp.zeros_like(theta[0]))
    gain = mpo_coef * mpo_on.astype(jnp.float32)
    rims = padded(env_left, (("bond", 0),), 1)
    share = states // lax.axis_size("bond")
    first = lax.axis_index("bond") * share
    count_all = lax.axis_size("sector") * states * states
    total = jnp.zeros((states, states), jnp.float32)
    for term_channel in range(bond_local):
        block = env_left[term_channel, 0]
        applied = jnp.dot(block, live, preferred_element_type=jnp.float32).astype(jnp.bfloat16)
        total = total + gain[term_channel] * lax.dot_general(
            applied,
            env_right[term_channel, 0],
            (((1,), (1,)), ((), ())),
            preferred_element_type=jnp.float32,
        )
    summed = lax.psum(total, "bond")
    product_full = summed * row_live[:, None] * col_live[None, :]
    square_total = lax.psum(jnp.sum(product_full * product_full), "sector")
    scale = lax.rsqrt(square_total / count_all + 1e-06)
    unit = (product_full * scale).astype(jnp.bfloat16)
    product_rows = lax.dynamic_slice_in_dim(product_full, first, share, 0)
    matvec = product_rows.astype(jnp.bfloat16)[None]
    table_index = jnp.arange(weight_table.shape[0], dtype=jnp.int32)
    mix_gain = jnp.sum(
        (mix_index[:, :, None] == table_index).astype(jnp.float32) * weight_table, axis=2
    )
    grown = []
    for channel in range(bond_local):
        mixed = (
            mix_gain[channel, 0] * rims[channel, 0].astype(jnp.float32)
            + mix_gain[channel, 1] * rims[channel + 1, 0].astype(jnp.float32)
            + mix_gain[channel, 2] * rims[channel + 2, 0].astype(jnp.float32)
        ).astype(jnp.bfloat16)
        half = jnp.dot(mixed, unit, preferred_element_type=jnp.float32).astype(jnp.bfloat16)
        outer = lax.dot_general(
            unit, half, (((0,), (0,)), ((), ())), preferred_element_type=jnp.float32
        )
        grown.append((outer / math.sqrt(states)).astype(jnp.bfloat16))
    env_next = jnp.stack(grown)[:, None]
    return (matvec, env_next)


def solution(mesh):
    in_specs = (
        P("sector", None, None),
        P("sector"),
        P("sector"),
        P("bond", "sector", None, None),
        P("bond", "sector", None, None),
        P("bond"),
        P("bond"),
        P("bond", None),
        P(),
    )
    out_specs = (P("sector", "bond", None), P("bond", "sector", None, None))
    return jax.shard_map(
        on_device, mesh=mesh, in_specs=in_specs, out_specs=out_specs, check_vma=False
    )
```

profile of v0, /device:TPU:0, one launch (start us, length us, event | category | flops | bytes accessed | tf_op | source)
XLA Modules:
  0.0 202.1 jit_solution(5226046945192987656)
XLA Ops:
  7.2 0.0 all-reduce.2.cloned.1.call-start
  8.5 0.7 convert_multiply_fusion.4
  9.2 0.6 fusion.62
  9.8 0.0 copy-start
  9.8 6.2 %fusion.15 = f32[768,768]{1,0:T(8,128)} fusion(bf16[2,1,768,768]{3,2,1,0:T(8,128)(2,1)} %param.13, bf16[1,768,768]{2,1,0:T(8,128)(2,1)} %param.9, pred[768]{0:T(1024)(128)(4,1)S(1)} %get-tuple-element.18, pred[768]{0:T(1024)(128)(4,1)S(1)} %get-tuple-element.19, bf16[2,1,768,768]{3,2,1,0:T(8,128)(2,1)} %param.12), kind=kOutput, calls=%fused_computation.29 | convolution fusion | flops 1813708800 | bytes 5899776 | tf_op jit(solution)/shard_map/dot_general | solution.py:42
  16.0 0.0 copy-done
  16.0 7.7 %multiply_add_fusion = f32[768,768]{1,0:T(8,128)} fusion(f32[768,768]{1,0:T(8,128)} %fusion.15, bf16[2,1,768,768]{3,2,1,0:T(8,128)(2,1)} %param.13, f32[]{:T(128)} %bitcast.6, f32[]{:T(128)} %bitcast, bf16[1,768,768]{2,1,0:T(8,128)(2,1)} %param.9, pred[768]{0:T(1024)(128)(4,1)S(1)} %get-tuple-element.18, pred[768]{0:T(1024)(128)(4,1)S(1)} %get-tuple-element.19, ...), kind=kOutput, calls=%fused_computation.16 | convolution fusion | flops 1815478272 | bytes 8260608 | tf_op jit(solution)/shard_map/dot_general | solution.py:42
  23.8 0.0 all-reduce.2.cloned.1.call-update
  23.8 0.0 copy-start.2
  23.8 0.0 copy-start.3
  23.8 1.2 fusion.60
  25.0 1.3 collective-permute-start.1
  26.3 6.5 %collective-permute-start = (bf16[1,1,768,768]{3,2,1,0:T(8,128)(2,1)S(1)}, bf16[1,1,768,768]{3,2,1,0:T(8,128)(2,1)}, u32[]{:S(2)}, u32[]{:S(2)}) collective-permute-start(bf16[1,1,768,768]{3,2,1,0:T(8,128)(2,1)S(1)} %get-tuple-element.8), channel_id=1, source_target_pairs={{0,4},{4,8},{8,12},{12,16},{16,20},{20,24},{24,28},{1,5},{5,9},{9,... | collective-permute-start | bytes 3538952 | tf_op jit(solution)/shard_map/ppermute | solution.py:16
  32.8 0.0 copy-done.2
  32.8 0.1 copy.12
  32.9 0.0 copy-done.3
  32.9 0.2 fusion.41
  33.1 0.6 fusion.61
  33.7 131.0 %all-reduce.2.cloned.1.call-done = f32[768,768]{1,0:T(8,128)} async-done(((f32[768,768]{1,0:T(8,128)}), f32[768,768]{1,0:T(8,128)}) %all-reduce.2.cloned.1.call-update) | async-done | bytes 2359312 | tf_op jit(solution)/shard_map/psum | solution.py:48
  164.6 3.1 %multiply_reduce_fusion = (f32[]{:T(128)}, f32[768,768]{1,0:T(8,128)S(1)}) fusion(f32[768]{0:T(1024)S(1)} %get-tuple-element.21, f32[768,768]{1,0:T(8,128)} %all-reduce.2.cloned.1.call-done, f32[768]{0:T(1024)S(1)} %get-tuple-element.20), kind=kLoop, calls=%fused_computation.14 | loop fusion | flops 2359295 | bytes 4724740 | tf_op jit(solution)/shard_map/reduce_sum | solution.py:50
  167.7 6.6 %psum.15 = f32[]{:T(128)} all-reduce(f32[]{:T(128)} %get-tuple-element.6), channel_id=1, replica_groups=mesh['bond'=8,'sector'=4] {'sector'}, use_global_device_ids=true, to_apply=%region_2.3 | all-reduce | flops 1 | bytes 8 | tf_op jit(solution)/shard_map/psum | solution.py:50
  175.0 0.7 fusion.40
  175.7 0.0 collective-permute-done.1
  175.7 8.3 %fusion.7 = bf16[1,768,768]{2,1,0:T(8,128)(2,1)} fusion(bf16[1,1,768,768]{3,2,1,0:T(8,128)(2,1)} %collective-permute-done.1, f32[]{:T(128)} %bitcast.17, f32[]{:T(128)} %bitcast.16, f32[]{:T(128)} %bitcast.15, f32[768,768]{1,0:T(8,128)S(1)} %get-tuple-element.7, f32[]{:T(128)S(6)} %rsqrt.3, bf16[2,1,768,768]{3,2,1,0:T(8,128)(2,1)} %param.12), kind=kOutput, calls=%fused_computation.23 | convolution fusion | flops 1821376512 | bytes 9438220 | tf_op jit(solution)/shard_map/dot_general | solution.py:67
  184.0 0.0 collective-permute-done
  184.0 0.0 copy-start.1
  184.0 8.4 %fusion.6 = bf16[1,768,768]{2,1,0:T(8,128)(2,1)} fusion(bf16[1,1,768,768]{3,2,1,0:T(8,128)(2,1)} %collective-permute-done, f32[]{:T(128)} %bitcast.13, f32[]{:T(128)} %bitcast.12, f32[]{:T(128)} %bitcast.10, f32[768,768]{1,0:T(8,128)S(1)} %get-tuple-element.7, f32[]{:T(128)S(6)} %rsqrt.3, bf16[2,1,768,768]{3,2,1,0:T(8,128)(2,1)} %param.12), kind=kOutput, calls=%fused_computation.22 | convolution fusion | flops 1821376512 | bytes 9438220 | tf_op jit(solution)/shard_map/dot_general | solution.py:67
  192.3 0.0 copy-done.1
  192.3 2.9 %maximum_bitcast_fusion = bf16[2,1,768,768]{3,2,1,0:T(8,128)(2,1)} fusion(bf16[1,768,768]{2,1,0:T(8,128)(2,1)S(1)} %copy-done.1, bf16[1,768,768]{2,1,0:T(8,128)(2,1)} %fusion.6), kind=kLoop, calls=%fused_computation.10 | loop fusion | flops 1179648 | bytes 4718592
  (2 shorter events, 0.0 us)
Async XLA Ops:
  7.2 157.5 %all-reduce.2.cloned.1.call-start = ((), (), s32[]{:S(2)}) async-start(), calls=%async_computation | async-start | bytes 4718592 | tf_op jit(solution)/shard_map/psum | solution.py:48
  9.8 6.3 %copy-start = (bf16[2,1,768,768]{3,2,1,0:T(8,128)(2,1)S(1)}, bf16[2,1,768,768]{3,2,1,0:T(8,128)(2,1)}, u32[]{:S(2)}) copy-start(bf16[2,1,768,768]{3,2,1,0:T(8,128)(2,1)} %param.12) | copy-start | bytes 7077892
  23.8 9.0 %copy-start.2 = (s32[2,3]{1,0:T(2,128)S(1)}, s32[2,3]{1,0:T(2,128)}, u32[]{:S(2)}) copy-start(s32[2,3]{1,0:T(2,128)} %param.16) | copy-start | bytes 76
  23.8 9.1 %copy-start.3 = (f32[8]{0:T(128)S(1)}, f32[8]{0:T(128)}, u32[]{:S(2)}) copy-start(f32[8]{0:T(128)} %param.17) | copy-start | bytes 100
  25.0 150.7 %collective-permute-start.1 = (bf16[1,1,768,768]{3,2,1,0:T(8,128)(2,1)}, bf16[1,1,768,768]{3,2,1,0:T(8,128)(2,1)}, u32[]{:S(2)}, u32[]{:S(2)}) collective-permute-start(bf16[1,1,768,768]{3,2,1,0:T(8,128)(2,1)} %get-tuple-element.9), channel_id=1, source_target_pairs={{4,0},{8,4},{12,8},{16,12},{20,16},{24,20},{28,24},{5,1},{9,5},{13... | collective-permute-start | bytes 3538952 | tf_op jit(solution)/shard_map/ppermute | solution.py:17
  26.3 157.7 %collective-permute-start = (bf16[1,1,768,768]{3,2,1,0:T(8,128)(2,1)S(1)}, bf16[1,1,768,768]{3,2,1,0:T(8,128)(2,1)}, u32[]{:S(2)}, u32[]{:S(2)}) collective-permute-start(bf16[1,1,768,768]{3,2,1,0:T(8,128)(2,1)S(1)} %get-tuple-element.8), channel_id=1, source_target_pairs={{0,4},{4,8},{8,12},{12,16},{16,20},{20,24},{24,28},{1,5},{5,9},{9,... | collective-permute-start | bytes 3538952 | tf_op jit(solution)/shard_map/ppermute | solution.py:16
  184.0 8.4 %copy-start.1 = (bf16[1,768,768]{2,1,0:T(8,128)(2,1)S(1)}, bf16[1,768,768]{2,1,0:T(8,128)(2,1)}, u32[]{:S(2)}) copy-start(bf16[1,768,768]{2,1,0:T(8,128)(2,1)} %fusion.7) | copy-start | bytes 3538948
Sparse Core Ops, SparseCore 0:
  23.9 140.6 all-reduce.1
where the time goes:
time: 202 us
  waiting for transfers between devices  131 us (65%)
  matrix products  30.6 us (15%)
  between operations  16 us (8%)
  starting transfers between devices  7.86 us (4%)
  other arithmetic  6.78 us (3%)
  blocking collectives  6.61 us (3%)
  local copies, waits for them, and re-layouts  3.18 us (2%)
    psum x1, waiting for transfers between devices, on_device(): summed = lax.psum(total, 'bond')  131 us
    dot_general x2, matrix products, on_device(): lax.dot_general(unit, half, (((0,), (0,)), ((), ())), preferred_element_t...  16.6 us
    dot_general x2, matrix products, on_device(): lax.dot_general(applied, env_right[term_channel, 0], (((1,), (1,)), ((),...  14 us
    psum x1, blocking collectives, on_device(): square_total = lax.psum(jnp.sum(product_full * product_full), 'sector')  6.61 us
    ppermute x1, starting transfers between devices, padded(): before = lax.ppermute(last, axis, up)  6.54 us
  transfers between devices with their start and end apart: 3, of which 1 were waited for; matrix products, arithmetic and copies ran while one was open for 7% of the time, Pallas kernels for 0%

commit v1 on v0

v1 whole, which is shorter than its diff:
```python
import functools
import math

import jax
import jax.numpy as jnp
from jax import lax
from jax.experimental import pallas as pl
from jax.experimental.pallas import tpu as pltpu
from jax.sharding import PartitionSpec as P

F32, BF16 = jnp.float32, jnp.bfloat16
SMEM = pl.BlockSpec(memory_space=pltpu.SMEM)
VMEM = pl.BlockSpec(memory_space=pltpu.VMEM)
NT = (((1,), (1,)), ((), ()))
TN = (((0,), (0,)), ((), ()))


def strip_of(states):
    return 256 if states % 256 == 0 else states


def partial_kernel(
    outer, inner, rows_ref, cols_ref, on_ref, coef_ref, theta_ref, left_ref, right_ref, out_ref, live, acc
):
    channel, last = pl.program_id(0), pl.num_programs(0) - 1
    states = theta_ref.shape[-1]
    share, strip = states // (outer * inner), strip_of(states)

    @pl.when(channel == 0)
    def _():
        row = lax.broadcasted_iota(jnp.int32, (states, states), 0)
        col = lax.broadcasted_iota(jnp.int32, (states, states), 1)
        keep = (row < rows_ref[0]) & (col < cols_ref[0])
        theta = theta_ref[0].astype(F32)
        live[...] = jnp.where(keep, theta, 0.0).astype(BF16)
        acc[...] = jnp.zeros_like(acc)

    gain = coef_ref[channel] * on_ref[channel].astype(F32)
    for at in range(0, states, strip):
        here = pl.ds(at, strip)
        applied = jnp.dot(left_ref[0, 0, here, :], live[...], preferred_element_type=F32).astype(BF16)
        term = lax.dot_general(applied, right_ref[0, 0], NT, preferred_element_type=F32)
        acc[here, :] += gain * term

    @pl.when(channel == last)
    def _():
        for hi in range(outer):
            for lo in range(inner):
                block = acc[pl.ds((hi * inner + lo) * share, share), :]
                out_ref[lo, pl.ds(hi * share, share), :] = block.astype(BF16)


def partial_sums(outer, inner, rows, cols, on, coef, theta, left, right):
    channels, states = left.shape[0], theta.shape[-1]
    block = pl.BlockSpec((1, 1, states, states), lambda c: (c, 0, 0, 0))
    whole = pl.BlockSpec((1, states, states), lambda c: (0, 0, 0))
    return pl.pallas_call(
        functools.partial(partial_kernel, outer, inner),
        name="partial_sums",
        grid=(channels,),
        out_shape=jax.ShapeDtypeStruct((inner, states // inner, states), BF16),
        in_specs=[SMEM, SMEM, SMEM, SMEM, whole, block, block],
        out_specs=pl.BlockSpec((inner, states // inner, states), lambda c: (0, 0, 0)),
        scratch_shapes=[pltpu.VMEM((states, states), BF16), pltpu.VMEM((states, states), F32)],
        cost_estimate=pl.CostEstimate(
            flops=4 * channels * states**3, bytes_accessed=4 * (channels + 1) * states**2, transcendentals=0
        ),
    )(rows, cols, on, coef, theta, left, right)


def grow_kernel(outer, inner, index_ref, table_ref, scale_ref, product_ref, own_ref, before_ref, after_ref, out_ref, unit, half):
    channels, states = own_ref.shape[0], own_ref.shape[-1]
    share, strip = states // (outer * inner), strip_of(states)
    scale = scale_ref[0]
    for hi in range(outer):
        for lo in range(inner):
            unit[pl.ds((hi * inner + lo) * share, share), :] = product_ref[lo, pl.ds(hi * share, share), :]
    around = [before_ref] + [own_ref.at[c, 0] for c in range(channels)] + [after_ref]
    for c in range(channels):
        for at in range(0, states, strip):
            here = pl.ds(at, strip)
            mixed = sum(
                table_ref[index_ref[c, k]] * around[c + k][here, :].astype(F32) for k in range(3)
            ).astype(BF16)
            first = jnp.dot(mixed, unit[...], preferred_element_type=F32)
            half[here, :] = (scale * first).astype(BF16)
        for at in range(0, states, strip):
            here = pl.ds(at, strip)
            second = lax.dot_general(unit[:, here], half[...], TN, preferred_element_type=F32)
            out_ref[c, 0, here, :] = (second * (scale * (1 / math.sqrt(states)))).astype(BF16)


def grow(outer, inner, index, table, scale, product, own, before, after):
    channels, states = own.shape[0], own.shape[-1]
    return pl.pallas_call(
        functools.partial(grow_kernel, outer, inner),
        name="grow",
        out_shape=jax.ShapeDtypeStruct(own.shape, BF16),
        in_specs=[SMEM, SMEM, SMEM, VMEM, VMEM, VMEM, VMEM],
        out_specs=VMEM,
        scratch_shapes=[pltpu.VMEM((states, states), BF16), pltpu.VMEM((states, states), BF16)],
        cost_estimate=pl.CostEstimate(
            flops=4 * channels * states**3, bytes_accessed=4 * (channels + 2) * states**2, transcendentals=0
        ),
    )(index, table, scale, product, own, before, after)


def rims(shard, axis):
    peers, length = lax.axis_size(axis), shard.shape[0]
    up = [(i, i + 1) for i in range(peers - 1)]
    down = [(j, i) for i, j in up]
    return lax.ppermute(shard[length - 1], axis, up), lax.ppermute(shard[0], axis, down)


def everyone(value, axes):
    for axis in axes:
        peers = lax.axis_size(axis)
        if peers & (peers - 1):
            value = lax.psum(value, axis)
            continue
        for bit in range(peers.bit_length() - 1):
            value = value + lax.ppermute(value, axis, [(i, i ^ (1 << bit)) for i in range(peers)])
    return value


def on_device(
    theta, sector_dims, right_dims, env_left, env_right, mpo_on, mpo_coef, mix_index, weight_table
):
  states = theta.shape[1]
  bonds, sectors = lax.axis_size("bond"), lax.axis_size("sector")
  share = states // bonds
  before, after = rims(env_left[:, 0], "bond")
  first = lax.axis_index("bond") * share
  count_all = sectors * states * states
  parts = partial_sums(bonds, 1, sector_dims, right_dims, mpo_on, mpo_coef, theta, env_left, env_right)
  met = lax.all_to_all(parts.reshape(bonds, share, states), "bond", 0, 0, tiled=True)
  rows = jnp.sum(met.astype(F32), axis=0)
  row_ids = first + jnp.arange(share, dtype=jnp.int32)
  keep = (row_ids < sector_dims[0])[:, None] & (jnp.arange(states, dtype=jnp.int32) < right_dims[0])[None, :]
  rows = jnp.where(keep, rows, 0.0)
  matvec = rows.astype(BF16)
  product = lax.all_to_all(jnp.broadcast_to(matvec[None], (bonds, share, states)), "bond", 0, 0, tiled=True)
  square_total = everyone(jnp.broadcast_to(jnp.sum(rows * rows), (1, 128)), ("sector", "bond"))[0, 0]
  scale = lax.rsqrt(square_total / count_all + 1e-06)
  grown = grow(bonds, 1, mix_index, weight_table, scale.reshape(1), product.reshape(1, states, states), env_left, before, after)
  return matvec[None], grown


def solution(mesh):
    in_specs = (
        P("sector", None, None),
        P("sector"),
        P("sector"),
        P("bond", "sector", None, None),
        P("bond", "sector", None, None),
        P("bond"),
        P("bond"),
        P("bond", None),
        P(),
    )
    out_specs = (P("sector", "bond", None), P("bond", "sector", None, None))
    return jax.shard_map(
        on_device, mesh=mesh, in_specs=in_specs, out_specs=out_specs, check_vma=False
    )
```

time: 202 us -> 134 us (0.66)
  waiting for transfers between devices: 131 us -> 80.7 us
  matrix products: 30.6 us -> 0 us
  starting transfers between devices: 7.86 us -> 28.6 us
  Pallas kernels: 0 us -> 15.9 us
  between operations: 16 us -> 2.13 us
  blocking collectives: 6.61 us -> 0 us
  other arithmetic: 6.78 us -> 3.1 us
    psum x1 -> x0, waiting for transfers between devices: 131 us -> none  [on_device(): summed = lax.psum(total, 'bond')]
    ppermute x2 -> x7, waiting for transfers between devices: 0.01 us -> 52.2 us  [the longest x5 52.2 us: everyone(): lax.ppermute(value, axis, [(i, i ^ 1 << bit) for i in range(peers)])]
    dot_general x4 -> x0, matrix products: 30.6 us -> none  [the longest x2 16.6 us: on_device(): lax.dot_general(unit, half, (((0,), (0,)), ((), ())), preferred_element_t...]
    all_to_all x0 -> x2, waiting for transfers between devices: none -> 28.6 us  [the longest x1 28.6 us: on_device(): lax.all_to_all(parts.reshape(bonds, share, states), 'bond', 0, 0, tiled=T...]
    pallas_call x0 -> x2, Pallas kernels: none -> 15.9 us  [the longest x1 8.01 us: grow(): pl.pallas_call(functools.partial(grow_kernel, outer, inner), name='grow',...]
    all_to_all x0 -> x2, starting transfers between devices: none -> 11.7 us  [the longest x1 7.28 us: on_device(): lax.all_to_all(parts.reshape(bonds, share, states), 'bond', 0, 0, tiled=T...]
    ppermute x2 -> x7, starting transfers between devices: 7.82 us -> 17 us  [the longest x5 10.1 us: everyone(): lax.ppermute(value, axis, [(i, i ^ 1 << bit) for i in range(peers)])]
    psum x1 -> x0, blocking collectives: 6.61 us -> none  [on_device(): square_total = lax.psum(jnp.sum(product_full * product_full), 'sector')]
  transfers between devices with their start and end apart: 3 -> 9, of which waited for: 1 -> 6; matrix products, arithmetic and copies ran while one was open for 7% -> 3% of each run, Pallas kernels for 0% -> 0%
where the time goes in v1:
time: 134 us; the launch traced here: 133 us
  waiting for transfers between devices  80.7 us (60%)
  starting transfers between devices  28.6 us (21%)
  Pallas kernels  15.9 us (12%)
  other arithmetic  3.1 us (2%)
  local copies, waits for them, and re-layouts  2.9 us (2%)
  between operations  2.13 us (2%)
    ppermute x5, waiting for transfers between devices, everyone(): lax.ppermute(value, axis, [(i, i ^ 1 << bit) for i in range(peers)])  52.2 us
    all_to_all x1, waiting for transfers between devices, on_device(): lax.all_to_all(parts.reshape(bonds, share, states), 'bond', 0, 0, tiled=T...  28.6 us
    ppermute x5, starting transfers between devices, everyone(): lax.ppermute(value, axis, [(i, i ^ 1 << bit) for i in range(peers)])  10.1 us
    pallas_call x1, Pallas kernels, grow(): pl.pallas_call(functools.partial(grow_kernel, outer, inner), name='grow',...  8.01 us
    pallas_call x1, Pallas kernels, partial_sums(): pl.pallas_call(functools.partial(partial_kernel, outer, inner), name='par...  7.89 us
    all_to_all x1, starting transfers between devices, on_device(): lax.all_to_all(parts.reshape(bonds, share, states), 'bond', 0, 0, tiled=T...  7.28 us
    ppermute x1, starting transfers between devices, rims(): lax.ppermute(shard[length - 1], axis, up)  5.6 us
    all_to_all x1, starting transfers between devices, on_device(): lax.all_to_all(jnp.broadcast_to(matvec[None], (bonds, share, states)), 'b...  4.38 us
  transfers between devices with their start and end apart: 9, of which 6 were waited for; matrix products, arithmetic and copies ran while one was open for 3% of the time, Pallas kernels for 0%

profile of v1, /device:TPU:0, one launch (start us, length us, event | category | flops | bytes accessed | tf_op | source)
XLA Modules:
  0.0 133.4 jit_solution(5274969669053126075)
XLA Ops:
  1.9 7.9 %partial_sums.1 = bf16[1,768,768]{2,1,0:T(8,128)(2,1)} custom-call(s32[1]{0:T(128)} %copy.11.rows_ref, s32[1]{0:T(128)} %copy.12.cols_ref, s32[2]{0:T(128)} %on_ref.1, f32[2]{0:T(128)} %coef_ref.1, bf16[1,768,768]{2,1,0:T(8,128)(2,1)} %theta_ref.1, bf16[2,1,768,768]{3,2,1,0:T(8,128)(2,1)} %own_ref.1, bf16[2,1,768,768]{3,2,1,0:T(8,128)(2,1)} %right_ref.1), custom_call_target="tpu_custom_call" | custom-call | flops 3623878656 | bytes 7077888 | tf_op jit(solution)/shard_map/partial_sums/pallas_call | solution.py:57
  9.8 7.3 %all-to-all-start = ((bf16[8,96,768]{2,1,0:T(8,128)(2,1)}), bf16[8,96,768]{2,1,0:T(8,128)(2,1)S(1)}, u32[]{:S(2)}, u32[]{:S(2)}) async-start(bf16[8,96,768]{2,1,0:T(8,128)(2,1)} %bitcast.16), calls=%async_computation | async-start | bytes 2359296 | tf_op jit(solution)/shard_map/all_to_all | solution.py:136
  17.1 28.6 %all-to-all-done = bf16[8,96,768]{2,1,0:T(8,128)(2,1)S(1)} async-done(((bf16[8,96,768]{2,1,0:T(8,128)(2,1)}), bf16[8,96,768]{2,1,0:T(8,128)(2,1)S(1)}, u32[]{:S(2)}, u32[]{:S(2)}) %all-to-all-start) | async-done | bytes 1179680 | tf_op jit(solution)/shard_map/all_to_all | solution.py:136
  45.7 0.2 convert_reduce_fusion
  45.8 0.1 fusion.1
  45.9 1.1 broadcast_in_dim.21
  47.0 4.4 %all-to-all-start.1 = ((bf16[8,96,768]{2,1,0:T(8,128)(2,1)}), bf16[8,96,768]{2,1,0:T(8,128)(2,1)}, u32[]{:S(2)}, u32[]{:S(2)}) async-start(bf16[8,96,768]{2,1,0:T(8,128)(2,1)} %broadcast_in_dim.21), calls=%async_computation.1 | async-start | bytes 2359296 | tf_op jit(solution)/shard_map/all_to_all | solution.py:142
  51.4 0.0 copy-done
  51.4 0.2 slice_bitcast_fusion
  51.6 1.3 collective-permute-start.6
  52.9 5.6 %collective-permute-start.5 = (bf16[768,768]{1,0:T(8,128)(2,1)S(1)}, bf16[768,768]{1,0:T(8,128)(2,1)}, u32[]{:S(2)}, u32[]{:S(2)}) collective-permute-start(bf16[768,768]{1,0:T(8,128)(2,1)S(1)} %get-tuple-element.3), channel_id=1, source_target_pairs={{0,4},{4,8},{8,12},{12,16},{16,20},{20,24},{24,28},{1,5},{5,9},{9,... | collective-permute-start | bytes 3538952 | tf_op jit(solution)/shard_map/ppermute | solution.py:112
  58.5 0.8 multiply_reduce_fusion
  59.3 0.6 broadcast_in_dim.20
  59.9 0.1 collective-permute-start
  60.0 1.1 collective-permute-done
  61.1 0.6 broadcast_add_fusion
  61.8 1.6 %collective-permute-start.1 = (f32[1,128]{1,0:T(1,128)S(1)}, f32[1,128]{1,0:T(1,128)S(1)}, u32[]{:S(2)}, u32[]{:S(2)}) collective-permute-start(f32[1,128]{1,0:T(1,128)S(1)} %broadcast_add_fusion), channel_id=1, source_target_pairs={{0,2},{1,3},{2,0},{3,1},{4,6},{5,7},{6,4},{7,5},{8,10},{9,11},{10,... | collective-permute-start | bytes 1544 | tf_op jit(solution)/shard_map/ppermute | solution.py:122
  63.4 2.0 %collective-permute-done.1 = f32[1,128]{1,0:T(1,128)S(1)} collective-permute-done((f32[1,128]{1,0:T(1,128)S(1)}, f32[1,128]{1,0:T(1,128)S(1)}, u32[]{:S(2)}, u32[]{:S(2)}) %collective-permute-start.1) | collective-permute-done | bytes 544 | tf_op jit(solution)/shard_map/ppermute | solution.py:122
  65.4 0.6 fusion.2
  66.1 1.8 %collective-permute-start.2 = (f32[1,128]{1,0:T(1,128)S(1)}, f32[1,128]{1,0:T(1,128)S(1)}, u32[]{:S(2)}, u32[]{:S(2)}) collective-permute-start(f32[1,128]{1,0:T(1,128)S(1)} %fusion.2), channel_id=1, source_target_pairs={{0,4},{4,0},{8,12},{12,8},{16,20},{20,16},{24,28},{28,24},{1,5},{5... | collective-permute-start | bytes 1544 | tf_op jit(solution)/shard_map/ppermute | solution.py:122
  67.9 46.5 %collective-permute-done.2 = f32[1,128]{1,0:T(1,128)S(1)} collective-permute-done((f32[1,128]{1,0:T(1,128)S(1)}, f32[1,128]{1,0:T(1,128)S(1)}, u32[]{:S(2)}, u32[]{:S(2)}) %collective-permute-start.2) | collective-permute-done | bytes 544 | tf_op jit(solution)/shard_map/ppermute | solution.py:122
  114.4 3.9 %collective-permute-start.3 = (f32[1,128]{1,0:T(1,128)S(1)}, f32[1,128]{1,0:T(1,128)S(1)}, u32[]{:S(2)}, u32[]{:S(2)}) collective-permute-start(f32[1,128]{1,0:T(1,128)S(1)} %add.33), channel_id=1, source_target_pairs={{0,8},{4,12},{8,0},{12,4},{16,24},{20,28},{24,16},{28,20},{1,9},{5... | collective-permute-start | bytes 1544 | tf_op jit(solution)/shard_map/ppermute | solution.py:122
  118.3 1.5 %collective-permute-done.3 = f32[1,128]{1,0:T(1,128)S(1)} collective-permute-done((f32[1,128]{1,0:T(1,128)S(1)}, f32[1,128]{1,0:T(1,128)S(1)}, u32[]{:S(2)}, u32[]{:S(2)}) %collective-permute-start.3) | collective-permute-done | bytes 544 | tf_op jit(solution)/shard_map/ppermute | solution.py:122
  119.8 2.8 %collective-permute-start.4 = (f32[1,128]{1,0:T(1,128)S(1)}, f32[1,128]{1,0:T(1,128)S(1)}, u32[]{:S(2)}, u32[]{:S(2)}) collective-permute-start(f32[1,128]{1,0:T(1,128)S(1)} %add.34), channel_id=1, source_target_pairs={{0,16},{4,20},{8,24},{12,28},{16,0},{20,4},{24,8},{28,12},{1,17},{... | collective-permute-start | bytes 1544 | tf_op jit(solution)/shard_map/ppermute | solution.py:122
  122.6 0.8 fusion
  123.3 0.9 collective-permute-done.4
  124.4 0.0 collective-permute-done.6.after_ref
  124.4 0.0 copy-start.1
  124.4 0.0 collective-permute-done.5.before_ref
  124.4 0.0 all-to-all-done.1
  124.4 1.0 copy-done.1
  125.4 8.0 %grow.1 = bf16[2,1,768,768]{3,2,1,0:T(8,128)(2,1)} custom-call(s32[2,3]{1,0:T(2,128)} %index_ref.1, f32[8]{0:T(128)} %table_ref.1, f32[1]{0:T(128)} %bitcast.4.scale_ref, bf16[1,768,768]{2,1,0:T(8,128)(2,1)} %bitcast.5.product_ref, bf16[2,1,768,768]{3,2,1,0:T(8,128)(2,1)} %own_ref.1, bf16[768,768]{1,0:T(8,128)(2,1)} %collective-permute-done.5.before_ref, ...), custom_call_target="tpu_custom_call" | custom-call | flops 3623878656 | bytes 9437184 | tf_op jit(solution)/shard_map/grow/pallas_call | solution.py:95
  (6 shorter events, 0.0 us)
Async XLA Ops:
  9.8 35.9 %all-to-all-start = ((bf16[8,96,768]{2,1,0:T(8,128)(2,1)}), bf16[8,96,768]{2,1,0:T(8,128)(2,1)S(1)}, u32[]{:S(2)}, u32[]{:S(2)}) async-start(bf16[8,96,768]{2,1,0:T(8,128)(2,1)} %bitcast.16), calls=%async_computation | async-start | bytes 2359296 | tf_op jit(solution)/shard_map/all_to_all | solution.py:136
  47.0 4.4 %copy-start = (bf16[2,1,768,768]{3,2,1,0:T(8,128)(2,1)S(1)}, bf16[2,1,768,768]{3,2,1,0:T(8,128)(2,1)}, u32[]{:S(2)}) copy-start(bf16[2,1,768,768]{3,2,1,0:T(8,128)(2,1)} %own_ref.1) | copy-start | bytes 7077892
  47.0 77.4 %all-to-all-start.1 = ((bf16[8,96,768]{2,1,0:T(8,128)(2,1)}), bf16[8,96,768]{2,1,0:T(8,128)(2,1)}, u32[]{:S(2)}, u32[]{:S(2)}) async-start(bf16[8,96,768]{2,1,0:T(8,128)(2,1)} %broadcast_in_dim.21), calls=%async_computation.1 | async-start | bytes 2359296 | tf_op jit(solution)/shard_map/all_to_all | solution.py:142
  51.6 72.8 %collective-permute-start.6 = (bf16[768,768]{1,0:T(8,128)(2,1)S(1)}, bf16[768,768]{1,0:T(8,128)(2,1)S(1)}, u32[]{:S(2)}, u32[]{:S(2)}) collective-permute-start(bf16[768,768]{1,0:T(8,128)(2,1)S(1)} %get-tuple-element.2), channel_id=1, source_target_pairs={{4,0},{8,4},{12,8},{16,12},{20,16},{24,20},{28,24},{5,1},{9,5},{13... | collective-permute-start | bytes 3538952 | tf_op jit(solution)/shard_map/ppermute | solution.py:112
  52.9 71.5 %collective-permute-start.5 = (bf16[768,768]{1,0:T(8,128)(2,1)S(1)}, bf16[768,768]{1,0:T(8,128)(2,1)}, u32[]{:S(2)}, u32[]{:S(2)}) collective-permute-start(bf16[768,768]{1,0:T(8,128)(2,1)S(1)} %get-tuple-element.3), channel_id=1, source_target_pairs={{0,4},{4,8},{8,12},{12,16},{16,20},{20,24},{24,28},{1,5},{5,9},{9,... | collective-permute-start | bytes 3538952 | tf_op jit(solution)/shard_map/ppermute | solution.py:112
  59.9 1.2 collective-permute-start
  61.8 3.6 %collective-permute-start.1 = (f32[1,128]{1,0:T(1,128)S(1)}, f32[1,128]{1,0:T(1,128)S(1)}, u32[]{:S(2)}, u32[]{:S(2)}) collective-permute-start(f32[1,128]{1,0:T(1,128)S(1)} %broadcast_add_fusion), channel_id=1, source_target_pairs={{0,2},{1,3},{2,0},{3,1},{4,6},{5,7},{6,4},{7,5},{8,10},{9,11},{10,... | collective-permute-start | bytes 1544 | tf_op jit(solution)/shard_map/ppermute | solution.py:122
  66.1 48.3 %collective-permute-start.2 = (f32[1,128]{1,0:T(1,128)S(1)}, f32[1,128]{1,0:T(1,128)S(1)}, u32[]{:S(2)}, u32[]{:S(2)}) collective-permute-start(f32[1,128]{1,0:T(1,128)S(1)} %fusion.2), channel_id=1, source_target_pairs={{0,4},{4,0},{8,12},{12,8},{16,20},{20,16},{24,28},{28,24},{1,5},{5... | collective-permute-start | bytes 1544 | tf_op jit(solution)/shard_map/ppermute | solution.py:122
  114.4 5.4 %collective-permute-start.3 = (f32[1,128]{1,0:T(1,128)S(1)}, f32[1,128]{1,0:T(1,128)S(1)}, u32[]{:S(2)}, u32[]{:S(2)}) collective-permute-start(f32[1,128]{1,0:T(1,128)S(1)} %add.33), channel_id=1, source_target_pairs={{0,8},{4,12},{8,0},{12,4},{16,24},{20,28},{24,16},{28,20},{1,9},{5... | collective-permute-start | bytes 1544 | tf_op jit(solution)/shard_map/ppermute | solution.py:122
  119.8 4.5 %collective-permute-start.4 = (f32[1,128]{1,0:T(1,128)S(1)}, f32[1,128]{1,0:T(1,128)S(1)}, u32[]{:S(2)}, u32[]{:S(2)}) collective-permute-start(f32[1,128]{1,0:T(1,128)S(1)} %add.34), channel_id=1, source_target_pairs={{0,16},{4,20},{8,24},{12,28},{16,0},{20,4},{24,8},{28,12},{1,17},{... | collective-permute-start | bytes 1544 | tf_op jit(solution)/shard_map/ppermute | solution.py:122
  124.4 1.0 copy-start.1

commit v2 on v1

v2 whole, which is shorter than its diff:
```python
import functools
import math

import jax
import jax.numpy as jnp
from jax import lax
from jax.experimental import pallas as pl
from jax.experimental.pallas import tpu as pltpu
from jax.sharding import PartitionSpec as P

F32, BF16 = jnp.float32, jnp.bfloat16
SMEM = pl.BlockSpec(memory_space=pltpu.SMEM)
VMEM = pl.BlockSpec(memory_space=pltpu.VMEM)
NT = (((1,), (1,)), ((), ()))


def strip_of(states):
    return 256 if states % 256 == 0 else states


def partial_kernel(
    outer, inner, rows_ref, cols_ref, on_ref, coef_ref, theta_ref, left_ref, right_ref, out_ref, live, acc
):
    channel, last = pl.program_id(0), pl.num_programs(0) - 1
    states = theta_ref.shape[-1]
    share, strip = states // (outer * inner), strip_of(states)

    @pl.when(channel == 0)
    def _():
        row = lax.broadcasted_iota(jnp.int32, (states, states), 0)
        col = lax.broadcasted_iota(jnp.int32, (states, states), 1)
        keep = (row < rows_ref[0]) & (col < cols_ref[0])
        theta = theta_ref[0].astype(F32)
        live[...] = jnp.where(keep, theta, 0.0).astype(BF16)
        acc[...] = jnp.zeros_like(acc)

    gain = coef_ref[channel] * on_ref[channel].astype(F32)
    for at in range(0, states, strip):
        here = pl.ds(at, strip)
        applied = jnp.dot(left_ref[0, 0, here, :], live[...], preferred_element_type=F32).astype(BF16)
        term = lax.dot_general(applied, right_ref[0, 0], NT, preferred_element_type=F32)
        acc[here, :] += gain * term

    @pl.when(channel == last)
    def _():
        for hi in range(outer):
            for lo in range(inner):
                block = acc[pl.ds((hi * inner + lo) * share, share), :]
                out_ref[lo, pl.ds(hi * share, share), :] = block.astype(BF16)


def partial_sums(outer, inner, rows, cols, on, coef, theta, left, right):
    channels, states = left.shape[0], theta.shape[-1]
    block = pl.BlockSpec((1, 1, states, states), lambda c: (c, 0, 0, 0))
    whole = pl.BlockSpec((1, states, states), lambda c: (0, 0, 0))
    return pl.pallas_call(
        functools.partial(partial_kernel, outer, inner),
        name="partial_sums",
        grid=(channels,),
        out_shape=jax.ShapeDtypeStruct((inner, states // inner, states), BF16),
        in_specs=[SMEM, SMEM, SMEM, SMEM, whole, block, block],
        out_specs=pl.BlockSpec((inner, states // inner, states), lambda c: (0, 0, 0)),
        scratch_shapes=[pltpu.VMEM((states, states), BF16), pltpu.VMEM((states, states), F32)],
        cost_estimate=pl.CostEstimate(
            flops=4 * channels * states**3, bytes_accessed=4 * (channels + 1) * states**2, transcendentals=0
        ),
    )(rows, cols, on, coef, theta, left, right)


LIFT = 2.0**40


def end_of(parity, channels, far):
    return jnp.where(far == 1, parity, 1 - parity) * (channels - 1)


def mix_rows(me_ref, index_ref, table_ref, own_ref, edges, mixed):
    far, parity, channels = pl.program_id(0), lax.rem(me_ref[0], 2), own_ref.shape[0]
    channel = end_of(parity, channels, far)
    step = (2 * far - 1) * (1 - 2 * parity)
    outward, centre, inward = (table_ref[index_ref[channel, k]] for k in (1 - step, 1, 1 + step))

    def mix(edge_ref):
        total = centre * own_ref[channel, 0].astype(F32) + inward * own_ref[channel + step, 0].astype(F32)
        mixed[...] = (total + outward * edge_ref[...].astype(F32)).astype(BF16)

    @pl.when(far == 0)
    def _():
        mix(edges[0])

    @pl.when(far == 1)
    def _():
        mix(edges[1])


def premix_kernel(me_ref, index_ref, table_ref, own_ref, near_ref, far_ref, out_ref):
    mix_rows(me_ref, index_ref, table_ref, own_ref, (near_ref, far_ref), out_ref.at[0])


def premix(me, index, table, own, near, far):
    channels, states, rows = own.shape[0], own.shape[-1], near.shape[0]
    edge = pl.BlockSpec((rows, states), lambda g: (0, 0))
    return pl.pallas_call(
        premix_kernel,
        name="premix",
        out_shape=jax.ShapeDtypeStruct((2, rows, states), BF16),
        grid=(2,),
        in_specs=[SMEM] * 3 + [pl.BlockSpec((channels, 1, rows, states), lambda g: (0, 0, 0, 0)), edge, edge],
        out_specs=pl.BlockSpec((1, rows, states), lambda g: (g, 0, 0)),
        cost_estimate=pl.CostEstimate(flops=12 * rows * states, bytes_accessed=12 * rows * states, transcendentals=0),
    )(me, index, table, own, near, far)


def turn_kernel(product_ref, turned_ref, square_ref):
    product = product_ref[...]
    wide = product.astype(F32)
    total = jnp.sum(jnp.sum(wide * wide, axis=0, keepdims=True), axis=1, keepdims=True)
    square_ref[...] = jnp.broadcast_to(total, square_ref.shape)
    turned_ref[...] = product.T


def turn(product):
    states = product.shape[-1]
    return pl.pallas_call(
        turn_kernel,
        name="turn",
        out_shape=[jax.ShapeDtypeStruct(product.shape, BF16), jax.ShapeDtypeStruct((8, 128), F32)],
        in_specs=[VMEM],
        out_specs=[VMEM, VMEM],
        cost_estimate=pl.CostEstimate(flops=2 * states**2, bytes_accessed=4 * states**2, transcendentals=0),
    )(product)


def early_kernel(product_ref, mixed_ref, out_ref):
    for g in range(2):
        first = jnp.dot(mixed_ref[g], product_ref[...], preferred_element_type=F32)
        out_ref[g] = (LIFT * first).astype(BF16)


def early(product, mixed):
    return pl.pallas_call(
        early_kernel,
        name="early",
        out_shape=jax.ShapeDtypeStruct(mixed.shape, BF16),
        in_specs=[VMEM, VMEM],
        out_specs=VMEM,
        cost_estimate=pl.CostEstimate(flops=2 * mixed.size * product.shape[0], bytes_accessed=6 * mixed.size, transcendentals=0),
    )(product, mixed)


def late_kernel(
    me_ref, index_ref, table_ref, scale_ref, product_ref, turned_ref, own_ref, early_ref, near_ref, far_ref, out_ref, mixed, half
):
    states, rows = product_ref.shape[-1], early_ref.shape[1]
    half[pl.ds(0, rows), :] = early_ref[0]
    mix_rows(me_ref, index_ref, table_ref, own_ref, (near_ref, far_ref), mixed)
    first = jnp.dot(mixed[...], product_ref[...], preferred_element_type=F32)
    half[pl.ds(rows, rows), :] = (LIFT * first).astype(BF16)
    factor = scale_ref[0] * scale_ref[0] * (1 / (LIFT * math.sqrt(states)))
    second = jnp.dot(turned_ref[...], half[...], preferred_element_type=F32)
    out_ref[0, 0] = (second * factor).astype(BF16)


def late(me, index, table, scale, product, turned, own, begun, near, far):
    channels, states, rows = own.shape[0], own.shape[-1], near.shape[0]
    edge = pl.BlockSpec((rows, states), lambda g, m: (0, 0))
    whole = pl.BlockSpec((states, states), lambda g, m: (0, 0))
    return pl.pallas_call(
        late_kernel,
        name="late",
        out_shape=jax.ShapeDtypeStruct(own.shape, BF16),
        grid_spec=pltpu.PrefetchScalarGridSpec(
            num_scalar_prefetch=1,
            grid=(2,),
            in_specs=[SMEM] * 3
            + [
                whole,
                whole,
                pl.BlockSpec((channels, 1, rows, states), lambda g, m: (0, 0, 1, 0)),
                pl.BlockSpec((1, rows, states), lambda g, m: (g, 0, 0)),
                edge,
                edge,
            ],
            out_specs=pl.BlockSpec(
                (1, 1, states, states), lambda g, m: (end_of(lax.rem(m[0], 2), channels, g), 0, 0, 0)
            ),
            scratch_shapes=[pltpu.VMEM((rows, states), BF16), pltpu.VMEM((states, states), BF16)],
        ),
        cost_estimate=pl.CostEstimate(flops=6 * states**3, bytes_accessed=16 * states**2, transcendentals=0),
    )(me, index, table, scale, product, turned, own, begun, near, far)


def everyone(value, axis):
    peers = lax.axis_size(axis)
    if peers & (peers - 1):
        return lax.psum(value, axis)
    terms = [value]
    for k in range(1, peers):
        terms.append(lax.ppermute(value, axis, [(i, i ^ k) for i in range(peers)]))
    while len(terms) > 1:
        terms = [a + b for a, b in zip(terms[::2], terms[1::2])]
    return terms[0]


def on_device(
    theta, sector_dims, right_dims, env_left, env_right, mpo_on, mpo_coef, mix_index, weight_table
):
    channels, states = env_left.shape[0], theta.shape[1]
    bonds, sectors = lax.axis_size("bond"), lax.axis_size("sector")
    share, cut = states // bonds, states // 2
    me = lax.axis_index("bond").astype(jnp.int32)
    pairs = {
        False: [(i, i ^ 1) for i in range(bonds) if i ^ 1 < bonds],
        True: [(i, (i + 1 ^ 1) - 1) for i in range(1, bonds) if (i + 1 ^ 1) - 1 < bonds],
    }

    def edge(source, far, at):
        end = end_of(me % 2, channels, int(far))
        slab = lax.dynamic_slice(source, (end, 0, at, 0), (1, 1, cut, states))[0, 0]
        return lax.ppermute(slab, "bond", pairs[far])

    near0 = edge(env_left, False, 0)
    far0 = edge(env_left, True, 0)
    parts = partial_sums(bonds, 1, sector_dims, right_dims, mpo_on, mpo_coef, theta, env_left, env_right)
    late_left, parts = lax.optimization_barrier((env_left, parts))
    met = lax.all_to_all(parts.reshape(bonds, share, states), "bond", 0, 0, tiled=True)
    near1 = edge(late_left, False, cut)
    far1 = edge(late_left, True, cut)
    rows = jnp.sum(met.astype(F32), axis=0)
    row_ids = me * share + jnp.arange(share, dtype=jnp.int32)
    keep = (row_ids < sector_dims[0])[:, None] & (jnp.arange(states, dtype=jnp.int32) < right_dims[0])[None, :]
    matvec = jnp.where(keep, rows, 0.0).astype(BF16)
    product = lax.all_to_all(jnp.broadcast_to(matvec[None], (bonds, share, states)), "bond", 0, 0, tiled=True)
    product = product.reshape(states, states)
    mixed = premix(jnp.reshape(me, (1,)), mix_index, weight_table, env_left, near0, far0)
    turned, square = turn(product)
    square_total = everyone(square, "sector")[0, 0]
    scale = lax.rsqrt(square_total / (sectors * states * states) + 1e-06).reshape(1)
    begun = early(product, mixed)
    grown = late(jnp.reshape(me, (1,)), mix_index, weight_table, scale, product, turned, env_left, begun, near1, far1)
    return matvec[None], grown


def solution(mesh):
    in_specs = (
        P("sector", None, None),
        P("sector"),
        P("sector"),
        P("bond", "sector", None, None),
        P("bond", "sector", None, None),
        P("bond"),
        P("bond"),
        P("bond", None),
        P(),
    )
    out_specs = (P("sector", "bond", None), P("bond", "sector", None, None))
    return jax.shard_map(
        on_device, mesh=mesh, in_specs=in_specs, out_specs=out_specs, check_vma=False
    )
```

time: 134 us -> 129 us (0.963); the launches traced: 133 us -> 127 us
  waiting for transfers between devices: 80.7 us -> 68.9 us
  Pallas kernels: 15.9 us -> 24.9 us
  starting transfers between devices: 28.6 us -> 23.2 us
  local copies, waits for them, and re-layouts: 2.9 us -> 6.2 us
  other arithmetic: 3.1 us -> 1.05 us
    ppermute x7, waiting for transfers between devices: 52.2 us -> 40.3 us  [the longest x4 40.3 us: edge(): return lax.ppermute(slab, 'bond', pairs[far])]
    pallas_call x1 -> x4, Pallas kernels: 8.01 us -> 17 us  [the longest x1 7.38 us: late(): pl.pallas_call(late_kernel, name='late', out_shape=jax.ShapeDtypeStruct(o...]
    ppermute x7, starting transfers between devices: 17 us -> 12.2 us  [the longest x4 10.3 us: edge(): return lax.ppermute(slab, 'bond', pairs[far])]
    unnamed x4 -> x18, local copies, waits for them, and re-layouts: 1 us -> 3.39 us
  transfers between devices with their start and end apart: 9 -> 9, of which waited for: 6 -> 2; matrix products, arithmetic and copies ran while one was open for 3% -> 2% of each run, Pallas kernels for 0% -> 8%
where the time goes in v2:
time: 129 us; the launch traced here: 127 us
  waiting for transfers between devices  68.9 us (53%)
  Pallas kernels  24.9 us (19%)
  starting transfers between devices  23.2 us (18%)
  local copies, waits for them, and re-layouts  6.2 us (5%)
  between operations  2.74 us (2%)
    ppermute x4, waiting for transfers between devices, edge(): return lax.ppermute(slab, 'bond', pairs[far])  40.3 us
    all_to_all x1, waiting for transfers between devices, on_device(): lax.all_to_all(parts.reshape(bonds, share, states), 'bond', 0, 0, tiled=T...  28.6 us
    ppermute x4, starting transfers between devices, edge(): return lax.ppermute(slab, 'bond', pairs[far])  10.3 us
    pallas_call x1, Pallas kernels, partial_sums(): pl.pallas_call(functools.partial(partial_kernel, outer, inner), name='par...  7.89 us
    pallas_call x1, Pallas kernels, late(): pl.pallas_call(late_kernel, name='late', out_shape=jax.ShapeDtypeStruct(o...  7.38 us
    all_to_all x1, starting transfers between devices, on_device(): lax.all_to_all(parts.reshape(bonds, share, states), 'bond', 0, 0, tiled=T...  7.28 us
    all_to_all x1, starting transfers between devices, on_device(): lax.all_to_all(jnp.broadcast_to(matvec[None], (bonds, share, states)), 'b...  3.77 us
    pallas_call x1, Pallas kernels, early(): pl.pallas_call(early_kernel, name='early', out_shape=jax.ShapeDtypeStruct...  3.74 us
  transfers between devices with their start and end apart: 9, of which 2 were waited for; matrix products, arithmetic and copies ran while one was open for 2% of the time, Pallas kernels for 8%

profile of v2, /device:TPU:0, one launch (start us, length us, event | category | flops | bytes accessed | tf_op | source)
XLA Modules:
  0.0 127.0 jit_solution(15157031825947355751)
XLA Ops:
  1.9 7.9 %partial_sums.1 = bf16[1,768,768]{2,1,0:T(8,128)(2,1)} custom-call(s32[1]{0:T(128)} %copy.11.rows_ref, s32[1]{0:T(128)} %copy.12.cols_ref, s32[2]{0:T(128)} %on_ref.1, f32[2]{0:T(128)} %coef_ref.1, bf16[1,768,768]{2,1,0:T(8,128)(2,1)} %theta_ref.1, bf16[2,1,768,768]{3,2,1,0:T(8,128)(2,1)} %own_ref.3, bf16[2,1,768,768]{3,2,1,0:T(8,128)(2,1)} %right_ref.1), custom_call_target="tpu_custom_call" | custom-call | flops 3623878656 | bytes 7077888 | tf_op jit(solution)/shard_map/partial_sums/pallas_call | solution.py:56
  9.8 7.3 %all-to-all-start = ((bf16[8,96,768]{2,1,0:T(8,128)(2,1)}), bf16[8,96,768]{2,1,0:T(8,128)(2,1)S(1)}, u32[]{:S(2)}, u32[]{:S(2)}) async-start(bf16[8,96,768]{2,1,0:T(8,128)(2,1)} %bitcast.23), calls=%async_computation | async-start | bytes 2359296 | tf_op jit(solution)/shard_map/all_to_all | solution.py:226
  17.1 28.6 %all-to-all-done = bf16[8,96,768]{2,1,0:T(8,128)(2,1)S(1)} async-done(((bf16[8,96,768]{2,1,0:T(8,128)(2,1)}), bf16[8,96,768]{2,1,0:T(8,128)(2,1)S(1)}, u32[]{:S(2)}, u32[]{:S(2)}) %all-to-all-start) | async-done | bytes 1179680 | tf_op jit(solution)/shard_map/all_to_all | solution.py:226
  45.7 0.2 convert_reduce_fusion
  45.8 0.0 copy-start.2
  45.8 0.1 select_convert_fusion
  46.0 0.5 copy-done.2
  46.5 1.1 broadcast_in_dim.17
  47.6 3.8 %all-to-all-start.1 = ((bf16[8,96,768]{2,1,0:T(8,128)(2,1)}), bf16[8,96,768]{2,1,0:T(8,128)(2,1)S(1)}, u32[]{:S(2)}, u32[]{:S(2)}) async-start(bf16[8,96,768]{2,1,0:T(8,128)(2,1)} %broadcast_in_dim.17), calls=%async_computation.1 | async-start | bytes 2359296 | tf_op jit(solution)/shard_map/all_to_all | solution.py:233
  51.4 0.1 dynamic-slice_bitcast_fusion.2
  51.5 0.7 collective-permute-start.4
  52.2 4.7 %collective-permute-start.3 = (bf16[384,768]{1,0:T(8,128)(2,1)S(1)}, bf16[384,768]{1,0:T(8,128)(2,1)S(1)}, u32[]{:S(2)}, u32[]{:S(2)}) collective-permute-start(bf16[384,768]{1,0:T(8,128)(2,1)S(1)} %get-tuple-element.13), channel_id=1, source_target_pairs={{0,4},{4,0},{8,12},{12,8},{16,20},{20,16},{24,28},{28,24},{1,5},{5... | collective-permute-start | bytes 1769480 | tf_op jit(solution)/shard_map/ppermute | solution.py:220
  56.9 1.1 dynamic-slice_bitcast_fusion
  58.0 0.7 collective-permute-start.6
  58.7 4.2 %collective-permute-start.5 = (bf16[384,768]{1,0:T(8,128)(2,1)}, bf16[384,768]{1,0:T(8,128)(2,1)S(1)}, u32[]{:S(2)}, u32[]{:S(2)}) collective-permute-start(bf16[384,768]{1,0:T(8,128)(2,1)} %get-tuple-element.11), channel_id=1, source_target_pairs={{0,4},{4,0},{8,12},{12,8},{16,20},{20,16},{24,28},{28,24},{1,5},{5... | collective-permute-start | bytes 1769480 | tf_op jit(solution)/shard_map/ppermute | solution.py:220
  62.9 0.0 collective-permute-done.4.far_ref
  62.9 40.3 %collective-permute-done.3.near_ref = bf16[384,768]{1,0:T(8,128)(2,1)S(1)} collective-permute-done((bf16[384,768]{1,0:T(8,128)(2,1)S(1)}, bf16[384,768]{1,0:T(8,128)(2,1)S(1)}, u32[]{:S(2)}, u32[]{:S(2)}) %collective-permute-start.3) | collective-permute-done | bytes 589856 | tf_op jit(solution)/shard_map/ppermute | solution.py:220
  103.2 0.8 copy-done.5
  104.0 3.2 %premix.1.mixed_ref = bf16[2,384,768]{2,1,0:T(8,128)(2,1)} custom-call(s32[1]{0:T(128)} %bitcast.4.me_ref, s32[2,3]{1,0:T(2,128)} %index_ref.3, f32[8]{0:T(128)} %table_ref.3, bf16[2,1,768,768]{3,2,1,0:T(8,128)(2,1)} %own_ref.3, bf16[384,768]{1,0:T(8,128)(2,1)} %copy-done.5, bf16[384,768]{1,0:T(8,128)(2,1)} %copy-done.4), custom_call_target="tpu_custom_call" | custom-call | flops 3538944 | bytes 3538944 | tf_op jit(solution)/shard_map/premix/pallas_call | solution.py:103
  107.2 0.8 fusion
  108.0 0.0 all-to-all-done.1
  108.0 1.0 copy-done
  109.0 2.7 %turn.1 = (bf16[768,768]{1,0:T(8,128)(2,1)}, f32[8,128]{1,0:T(8,128)}) custom-call(bf16[768,768]{1,0:T(8,128)(2,1)} %bitcast.20), custom_call_target="tpu_custom_call" | custom-call | flops 1179648 | bytes 2359296 | tf_op jit(solution)/shard_map/turn/pallas_call | solution.py:124
  111.7 0.0 collective-permute-start.2
  111.8 1.5 %collective-permute-start.1 = (f32[8,128]{1,0:T(8,128)}, f32[8,128]{1,0:T(8,128)S(1)}, u32[]{:S(2)}, u32[]{:S(2)}) collective-permute-start(f32[8,128]{1,0:T(8,128)} %get-tuple-element.7), channel_id=1, source_target_pairs={{0,2},{1,3},{2,0},{3,1},{4,6},{5,7},{6,4},{7,5},{8,10},{9,11},{10,... | collective-permute-start | bytes 12296 | tf_op jit(solution)/shard_map/ppermute | solution.py:199
  113.3 0.3 collective-permute-start
  113.6 3.7 %early.1.early_ref = bf16[2,384,768]{2,1,0:T(8,128)(2,1)} custom-call(bf16[768,768]{1,0:T(8,128)(2,1)} %bitcast.21, bf16[2,384,768]{2,1,0:T(8,128)(2,1)} %premix.1.mixed_ref), custom_call_target="tpu_custom_call" | custom-call | flops 905969664 | bytes 3538944 | tf_op jit(solution)/shard_map/early/pallas_call | solution.py:141
  117.4 0.5 slice.3
  118.6 0.0 collective-permute-done.6.far_ref
  118.6 0.8 copy-done.7
  119.4 0.2 copy-done.8
  119.6 7.4 %late.1 = bf16[2,1,768,768]{3,2,1,0:T(8,128)(2,1)} custom-call(s32[1]{0:T(128)} %bitcast.4.me_ref, s32[2,3]{1,0:T(2,128)} %index_ref.3, f32[8]{0:T(128)} %table_ref.3, f32[1]{0:T(128)} %bitcast.6.scale_ref, bf16[768,768]{1,0:T(8,128)(2,1)} %bitcast.22, bf16[768,768]{1,0:T(8,128)(2,1)} %get-tuple-element.8.turned_ref, bf16[2,1,768,768]{3,2,1,0:T(8,128)(2,1)} %own_ref.3, ...), custom_call_target="tpu_custom_call" | custom-call | flops 2717908992 | bytes 9437184 | tf_op jit(solution)/shard_map/late/pallas_call | solution.py:168
  (19 shorter events, 0.1 us)
Async XLA Ops:
  9.8 35.9 %all-to-all-start = ((bf16[8,96,768]{2,1,0:T(8,128)(2,1)}), bf16[8,96,768]{2,1,0:T(8,128)(2,1)S(1)}, u32[]{:S(2)}, u32[]{:S(2)}) async-start(bf16[8,96,768]{2,1,0:T(8,128)(2,1)} %bitcast.23), calls=%async_computation | async-start | bytes 2359296 | tf_op jit(solution)/shard_map/all_to_all | solution.py:226
  45.8 0.7 copy-start.2
  47.6 3.8 %copy-start.1 = (bf16[2,1,768,768]{3,2,1,0:T(8,128)(2,1)S(1)}, bf16[2,1,768,768]{3,2,1,0:T(8,128)(2,1)}, u32[]{:S(2)}) copy-start(bf16[2,1,768,768]{3,2,1,0:T(8,128)(2,1)} %own_ref.3) | copy-start | bytes 7077892
  47.6 60.4 %all-to-all-start.1 = ((bf16[8,96,768]{2,1,0:T(8,128)(2,1)}), bf16[8,96,768]{2,1,0:T(8,128)(2,1)S(1)}, u32[]{:S(2)}, u32[]{:S(2)}) async-start(bf16[8,96,768]{2,1,0:T(8,128)(2,1)} %broadcast_in_dim.17), calls=%async_computation.1 | async-start | bytes 2359296 | tf_op jit(solution)/shard_map/all_to_all | solution.py:233
  51.5 11.5 %collective-permute-start.4 = (bf16[384,768]{1,0:T(8,128)(2,1)S(1)}, bf16[384,768]{1,0:T(8,128)(2,1)S(1)}, u32[]{:S(2)}, u32[]{:S(2)}) collective-permute-start(bf16[384,768]{1,0:T(8,128)(2,1)S(1)} %get-tuple-element.12), channel_id=1, source_target_pairs={{4,8},{8,4},{12,16},{16,12},{20,24},{24,20},{5,9},{9,5},{13,17},{1... | collective-permute-start | bytes 1769480 | tf_op jit(solution)/shard_map/ppermute | solution.py:220
  52.2 51.0 %collective-permute-start.3 = (bf16[384,768]{1,0:T(8,128)(2,1)S(1)}, bf16[384,768]{1,0:T(8,128)(2,1)S(1)}, u32[]{:S(2)}, u32[]{:S(2)}) collective-permute-start(bf16[384,768]{1,0:T(8,128)(2,1)S(1)} %get-tuple-element.13), channel_id=1, source_target_pairs={{0,4},{4,0},{8,12},{12,8},{16,20},{20,16},{24,28},{28,24},{1,5},{5... | collective-permute-start | bytes 1769480 | tf_op jit(solution)/shard_map/ppermute | solution.py:220
  58.0 60.6 %collective-permute-start.6 = (bf16[384,768]{1,0:T(8,128)(2,1)}, bf16[384,768]{1,0:T(8,128)(2,1)S(1)}, u32[]{:S(2)}, u32[]{:S(2)}) collective-permute-start(bf16[384,768]{1,0:T(8,128)(2,1)} %get-tuple-element.10), channel_id=1, source_target_pairs={{4,8},{8,4},{12,16},{16,12},{20,24},{24,20},{5,9},{9,5},{13,17},{1... | collective-permute-start | bytes 1769480 | tf_op jit(solution)/shard_map/ppermute | solution.py:220
  58.7 59.9 %collective-permute-start.5 = (bf16[384,768]{1,0:T(8,128)(2,1)}, bf16[384,768]{1,0:T(8,128)(2,1)S(1)}, u32[]{:S(2)}, u32[]{:S(2)}) collective-permute-start(bf16[384,768]{1,0:T(8,128)(2,1)} %get-tuple-element.11), channel_id=1, source_target_pairs={{0,4},{4,0},{8,12},{12,8},{16,20},{20,16},{24,28},{28,24},{1,5},{5... | collective-permute-start | bytes 1769480 | tf_op jit(solution)/shard_map/ppermute | solution.py:220
  62.9 40.3 %copy-start.4 = (bf16[384,768]{1,0:T(8,128)(2,1)}, bf16[384,768]{1,0:T(8,128)(2,1)S(1)}, u32[]{:S(2)}) copy-start(bf16[384,768]{1,0:T(8,128)(2,1)S(1)} %collective-permute-done.4.far_ref) | copy-start | bytes 1769476
  103.2 0.8 copy-start.5
  104.0 3.2 %copy-start.3 = (bf16[96,768]{1,0:T(8,128)(2,1)S(1)}, bf16[96,768]{1,0:T(8,128)(2,1)}, u32[]{:S(2)}) copy-start(bf16[96,768]{1,0:T(8,128)(2,1)} %copy-done.2) | copy-start | bytes 442372
  108.0 1.0 copy-start
  111.7 5.6 %copy-start.6 = (f32[8,128]{1,0:T(8,128)S(1)}, f32[8,128]{1,0:T(8,128)}, u32[]{:S(2)}) copy-start(f32[8,128]{1,0:T(8,128)} %get-tuple-element.7) | copy-start | bytes 12292
  111.7 5.6 %collective-permute-start.2 = (f32[8,128]{1,0:T(8,128)}, f32[8,128]{1,0:T(8,128)S(1)}, u32[]{:S(2)}, u32[]{:S(2)}) collective-permute-start(f32[8,128]{1,0:T(8,128)} %get-tuple-element.7), channel_id=1, source_target_pairs={{0,3},{1,2},{2,1},{3,0},{4,7},{5,6},{6,5},{7,4},{8,11},{9,10},{10,... | collective-permute-start | bytes 12296 | tf_op jit(solution)/shard_map/ppermute | solution.py:199
  111.8 5.6 %collective-permute-start.1 = (f32[8,128]{1,0:T(8,128)}, f32[8,128]{1,0:T(8,128)S(1)}, u32[]{:S(2)}, u32[]{:S(2)}) collective-permute-start(f32[8,128]{1,0:T(8,128)} %get-tuple-element.7), channel_id=1, source_target_pairs={{0,2},{1,3},{2,0},{3,1},{4,6},{5,7},{6,4},{7,5},{8,10},{9,11},{10,... | collective-permute-start | bytes 12296 | tf_op jit(solution)/shard_map/ppermute | solution.py:199
  113.3 4.1 %collective-permute-start = (f32[8,128]{1,0:T(8,128)}, f32[8,128]{1,0:T(8,128)S(1)}, u32[]{:S(2)}, u32[]{:S(2)}) collective-permute-start(f32[8,128]{1,0:T(8,128)} %get-tuple-element.7), channel_id=1, source_target_pairs={{0,1},{1,0},{2,3},{3,2},{4,5},{5,4},{6,7},{7,6},{8,9},{9,8},{10,11... | collective-permute-start | bytes 12296 | tf_op jit(solution)/shard_map/ppermute | solution.py:199
  118.6 0.8 copy-start.7
  118.6 1.0 copy-start.8
